TPU v7x, 32 devices: a whole 2x2x4 slice. The times are simulated.
32 devices in a mesh: dp: 8 (over z, y), grp: 4 (over x, core).
Axes of the slice: x: 2, y: 2, z: 4, core: 2. Of those that a mesh axis runs over, the one named last changes fastest.
Arguments:
- activations: bfloat16 [32, 512, 768], P('dp', None, 'grp'), may hold values from -6 to 6, as said below
- cotangent: bfloat16 [32, 512, 768], P('dp', None, 'grp'), may hold values from -6 to 6
- lengths: int32 [32], P('dp'), may hold values from 64 to 512
- triple_weight: bfloat16 [2, 4, 192, 576], P(None, 'grp'), may hold values from -0.25980762 to 0.25980762, as said below
- triple_bias: float32 [2, 2, 768], P(None, None, 'grp'), may hold values from -1.8 to 1.8, as said below
- output_weight: bfloat16 [2, 768, 768], replicated, may hold values from -1.75 to 1.75
- output_bias: float32 [2, 768], replicated, may hold values from -1.75 to 1.75
- first_gain: float32 [2, 768], replicated, may hold values from 0.25 to 1.75
- first_shift: float32 [2, 768], replicated, may hold values from -1.75 to 1.75
- widen_weight: bfloat16 [2, 4, 192, 768], P(None, 'grp'), may hold values from -0.4375 to 0.4375
- widen_bias: float32 [2, 3072], P(None, 'grp'), may hold values from -1.75 to 1.75
- shrink_weight: bfloat16 [2, 4, 768, 192], P(None, 'grp'), may hold values from -0.21875 to 0.21875
- narrow_bias: float32 [2, 768], P(None, 'grp'), may hold values from -1.75 to 1.75
- second_gain: float32 [2, 768], P(None, 'grp'), may hold values from 0.25 to 1.75
- second_shift: float32 [2, 768], P(None, 'grp'), may hold values from -1.75 to 1.75
Outputs:
- layer_output: bfloat16 [32, 512, 768], P('dp', None, 'grp')
- input_gradient: float32 [32, 512, 768], P('dp', None, 'grp')
- triple_weight_gradient: float32 [2, 4, 192, 576], P(None, 'grp')
- triple_bias_gradient: float32 [2, 2, 768], P(None, None, 'grp')
- output_weight_gradient: float32 [2, 768, 768], replicated
- output_bias_gradient: float32 [2, 768], replicated
- first_gain_gradient: float32 [2, 768], replicated
- first_shift_gradient: float32 [2, 768], replicated
- widen_weight_gradient: float32 [2, 4, 192, 768], P(None, 'grp')
- widen_bias_gradient: float32 [2, 3072], P(None, 'grp')
- narrow_weight_gradient: float32 [2, 4, 768, 192], P(None, 'grp')
- narrow_bias_gradient: float32 [2, 768], P(None, 'grp')
- second_norm_gain_gradient: float32 [2, 768], P(None, 'grp')
- second_shift_gradient: float32 [2, 768], P(None, 'grp')
Inputs may be any that keep to these rules, and one draw needn't show every extreme that they name: `activations`: independent entries of order one. `triple_weight`: independent entries with deviation about 192 ** -0.5. `triple_bias`: independent entries with deviation about 0.3.
All inputs are finite; a program needn't handle non-finite values.
Results may differ from a plain program's by a relative error of at most 0.015.
Values may be sent and summed in bfloat16 or wider, within the bound.
A program may use at most 192 MiB of HBM per device.

v0:
```python
import math
import jax
import jax.numpy as jnp
from jax import lax
from jax.sharding import PartitionSpec as P

HEAD = 64
EPSILON = 1e-05
MASKED = -1e30


def contract_rows(left, right):
    return lax.dot_general(
        left, right, (((0,), (0,)), ((), ())), preferred_element_type=jnp.float32
    )


def contract_cols(left, weight):
    return lax.dot_general(
        left, weight, (((1,), (1,)), ((), ())), preferred_element_type=jnp.float32
    )


def split_heads(block):
    return block.reshape(block.shape[0], block.shape[1] // HEAD, HEAD)


def score_block(queries, keys, length):
    scores = jnp.einsum(
        "qhd,khd->hqk", split_heads(queries), split_heads(keys), preferred_element_type=jnp.float32
    ) * HEAD ** (-0.5)
    visible = jnp.arange(keys.shape[0]) < length
    return jnp.where(visible[None, None, :], scores, MASKED)


def attend_forward(queries, keys, values, lengths):

    def single(inputs):
        query_one, key_one, value_one, length = inputs
        scores = score_block(query_one, key_one, length)
        highest = jnp.max(scores, axis=-1, keepdims=True)
        expon = jnp.exp(scores - highest)
        totals = jnp.sum(expon, axis=-1, keepdims=True)
        weights = (expon / totals).astype(jnp.bfloat16)
        mixed = jnp.einsum(
            "hqk,khd->qhd", weights, split_heads(value_one), preferred_element_type=jnp.float32
        )
        return (mixed.reshape(query_one.shape).astype(jnp.bfloat16), highest, totals)

    return lax.map(single, (queries, keys, values, lengths))


def attend_backward(queries, keys, values, outgrad, highest, totals, lengths):

    def single(inputs):
        query_one, key_one, value_one, grad_one, top, total, length = inputs
        scores = score_block(query_one, key_one, length)
        probs = jnp.exp(scores - top) / total
        weights = probs.astype(jnp.bfloat16)
        grad_heads = split_heads(grad_one)
        grad_probs = jnp.einsum(
            "qhd,khd->hqk", grad_heads, split_heads(value_one), preferred_element_type=jnp.float32
        )
        inner = jnp.sum(probs * grad_probs, axis=-1, keepdims=True)
        grad_scores = (probs * (grad_probs - inner)).astype(jnp.bfloat16)
        factor = HEAD ** (-0.5)
        query_grad = (
            jnp.einsum(
                "hqk,khd->qhd",
                grad_scores,
                split_heads(key_one),
                preferred_element_type=jnp.float32,
            )
            * factor
        )
        key_grad = (
            jnp.einsum(
                "hqk,qhd->khd",
                grad_scores,
                split_heads(query_one),
                preferred_element_type=jnp.float32,
            )
            * factor
        )
        value_grad = jnp.einsum(
            "hqk,qhd->khd", weights, grad_heads, preferred_element_type=jnp.float32
        )
        shape = query_one.shape
        return (
            query_grad.reshape(shape).astype(jnp.bfloat16),
            key_grad.reshape(shape).astype(jnp.bfloat16),
            value_grad.reshape(shape).astype(jnp.bfloat16),
        )

    return lax.map(single, (queries, keys, values, outgrad, highest, totals, lengths))


def gelu_slope(values):
    return 0.5 * (1.0 + lax.erf(values / math.sqrt(2.0))) + values * jnp.exp(
        -0.5 * values * values
    ) / math.sqrt(2.0 * math.pi)


def layer_forward(inputs, lengths, params, layer_params):
    (
        triple_weight,
        triple_bias,
        output_weight,
        output_bias,
        first_gain,
        first_shift,
        widen_weight,
        widen_bias,
        shrink_weight,
        narrow_bias,
        second_gain,
        second_shift,
    ) = params
    group_width = inputs.shape[-1]
    rows = inputs.reshape(-1, group_width)
    projected = jnp.dot(rows, triple_weight[layer_params, 0], preferred_element_type=jnp.float32)
    queries = (
        (projected[:, :group_width] + triple_bias[layer_params, 0])
        .astype(jnp.bfloat16)
        .reshape(inputs.shape)
    )
    keys = projected[:, group_width : 2 * group_width].astype(jnp.bfloat16).reshape(inputs.shape)
    values = (
        (projected[:, 2 * group_width :] + triple_bias[layer_params, 1])
        .astype(jnp.bfloat16)
        .reshape(inputs.shape)
    )
    queries, keys, values, residual = (
        lax.all_to_all(queries, "grp", split_axis=0, concat_axis=2, tiled=True),
        lax.all_to_all(keys, "grp", split_axis=0, concat_axis=2, tiled=True),
        lax.all_to_all(values, "grp", split_axis=0, concat_axis=2, tiled=True),
        lax.all_to_all(inputs, "grp", split_axis=0, concat_axis=2, tiled=True),
    )
    local = queries.shape[0]
    mine = lax.dynamic_slice_in_dim(lengths, lax.axis_index("grp") * local, local)
    attended, highest, totals = attend_forward(queries, keys, values, mine)
    width = attended.shape[-1]
    flat = attended.reshape(-1, width)
    before = (
        residual.reshape(-1, width).astype(jnp.float32)
        + jnp.dot(flat, output_weight[layer_params], preferred_element_type=jnp.float32)
        + output_bias[layer_params]
    )
    center = before - jnp.mean(before, axis=-1, keepdims=True)
    first_inverse = lax.rsqrt(jnp.mean(center * center, axis=-1, keepdims=True) + EPSILON)
    first_normed = center * first_inverse
    hidden = (
        (first_normed * first_gain[layer_params] + first_shift[layer_params])
        .astype(jnp.bfloat16)
        .reshape(attended.shape)
    )
    hidden_group = lax.all_to_all(hidden, "grp", split_axis=2, concat_axis=0, tiled=True)
    group_rows = hidden_group.reshape(-1, group_width)
    widened = (
        jnp.dot(group_rows, widen_weight[layer_params, 0], preferred_element_type=jnp.float32)
        + widen_bias[layer_params]
    )
    gelu_output = jax.nn.gelu(widened, approximate=False).astype(jnp.bfloat16)
    after = (
        group_rows.astype(jnp.float32)
        + jnp.dot(gelu_output, shrink_weight[layer_params, 0], preferred_element_type=jnp.float32)
        + narrow_bias[layer_params]
    )
    row_sum = jnp.sum(after, axis=-1)
    row_square = jnp.sum(after * after, axis=-1)
    total_sum, total_square = lax.psum((row_sum, row_square), "grp")
    average = (total_sum / width)[:, None]
    variance = (total_square / width)[:, None] - average * average
    second_inverse = lax.rsqrt(variance + EPSILON)
    second_normed = (after - average) * second_inverse
    output = (second_normed * second_gain[layer_params] + second_shift[layer_params]).reshape(
        inputs.shape
    )
    kept = (
        inputs,
        queries,
        keys,
        values,
        mine,
        highest,
        totals,
        attended,
        first_normed,
        first_inverse,
        group_rows,
        widened,
        gelu_output,
        second_normed,
        second_inverse,
    )
    return (output, kept)


def layer_backward(outgrad, params, layer_params, kept):
    (
        triple_weight,
        triple_bias,
        output_weight,
        output_bias,
        first_gain,
        first_shift,
        widen_weight,
        widen_bias,
        shrink_weight,
        narrow_bias,
        second_gain,
        second_shift,
    ) = params
    (
        inputs,
        queries,
        keys,
        values,
        mine,
        highest,
        totals,
        attended,
        first_normed,
        first_inverse,
        group_rows,
        widened,
        gelu_output,
        second_normed,
        second_inverse,
    ) = kept
    group_width = inputs.shape[-1]
    width = attended.shape[-1]
    grad_rows = outgrad.reshape(-1, group_width)
    scaled = grad_rows * second_gain[layer_params]
    part_sum = jnp.sum(scaled, axis=-1)
    part_cross = jnp.sum(scaled * second_normed, axis=-1)
    total_sum, total_cross = lax.psum((part_sum, part_cross), "grp")
    grad_after = second_inverse * (
        scaled - (total_sum / width)[:, None] - second_normed * (total_cross / width)[:, None]
    )
    second_gain_grad = jnp.sum(grad_rows * second_normed, axis=0)
    second_shift_grad = jnp.sum(grad_rows, axis=0)
    narrow_rounded = grad_after.astype(jnp.bfloat16)
    narrow_weight_grad = contract_rows(gelu_output, narrow_rounded)
    narrow_bias_grad = jnp.sum(narrow_rounded.astype(jnp.float32), axis=0)
    gelu_output_gradient = contract_cols(narrow_rounded, shrink_weight[layer_params, 0])
    widened_grad = (gelu_output_gradient * gelu_slope(widened)).astype(jnp.bfloat16)
    widen_weight_grad = contract_rows(group_rows, widened_grad)
    widen_bias_grad = jnp.sum(widened_grad.astype(jnp.float32), axis=0)
    hidden_grad = (grad_after + contract_cols(widened_grad, widen_weight[layer_params, 0])).astype(
        jnp.bfloat16
    )
    hidden_seq = lax.all_to_all(
        hidden_grad.reshape(inputs.shape), "grp", split_axis=0, concat_axis=2, tiled=True
    )
    seq_rows = hidden_seq.reshape(-1, width).astype(jnp.float32)
    first_gain_grad = jnp.sum(seq_rows * first_normed, axis=0)
    first_shift_grad = jnp.sum(seq_rows, axis=0)
    scaled_first = seq_rows * first_gain[layer_params]
    grad_before = first_inverse * (
        scaled_first
        - jnp.mean(scaled_first, axis=-1, keepdims=True)
        - first_normed * jnp.mean(scaled_first * first_normed, axis=-1, keepdims=True)
    )
    before_rounded = grad_before.astype(jnp.bfloat16)
    flat = attended.reshape(-1, width)
    output_weight_grad = contract_rows(flat, before_rounded)
    output_bias_grad = jnp.sum(before_rounded.astype(jnp.float32), axis=0)
    attended_grad = (
        contract_cols(before_rounded, output_weight[layer_params])
        .astype(jnp.bfloat16)
        .reshape(attended.shape)
    )
    residual_grad = before_rounded.reshape(attended.shape)
    query_seq, key_seq, value_seq = attend_backward(
        queries, keys, values, attended_grad, highest, totals, mine
    )
    query_grad, key_grad, value_grad, input_part = (
        lax.all_to_all(query_seq, "grp", split_axis=2, concat_axis=0, tiled=True),
        lax.all_to_all(key_seq, "grp", split_axis=2, concat_axis=0, tiled=True),
        lax.all_to_all(value_seq, "grp", split_axis=2, concat_axis=0, tiled=True),
        lax.all_to_all(residual_grad, "grp", split_axis=2, concat_axis=0, tiled=True),
    )
    triple_grad = jnp.concatenate(
        [
            query_grad.reshape(-1, group_width),
            key_grad.reshape(-1, group_width),
            value_grad.reshape(-1, group_width),
        ],
        axis=-1,
    )
    triple_weight_grad = contract_rows(inputs.reshape(-1, group_width), triple_grad)
    triple_bias_grad = jnp.stack(
        [
            jnp.sum(query_grad.reshape(-1, group_width).astype(jnp.float32), axis=0),
            jnp.sum(value_grad.reshape(-1, group_width).astype(jnp.float32), axis=0),
        ]
    )
    input_grad = contract_cols(triple_grad, triple_weight[layer_params, 0]) + input_part.reshape(
        -1, group_width
    ).astype(jnp.float32)
    grads = (
        triple_weight_grad[None],
        triple_bias_grad,
        output_weight_grad,
        output_bias_grad,
        first_gain_grad,
        first_shift_grad,
        widen_weight_grad[None],
        widen_bias_grad,
        narrow_weight_grad[None],
        narrow_bias_grad,
        second_gain_grad,
        second_shift_grad,
    )
    return (input_grad.reshape(inputs.shape), grads)


def shards(
    activations,
    cotangent,
    lengths,
    triple_weight,
    triple_bias,
    output_weight,
    output_bias,
    first_gain,
    first_shift,
    widen_weight,
    widen_bias,
    shrink_weight,
    narrow_bias,
    second_gain,
    second_shift,
):
    params = (
        triple_weight,
        triple_bias,
        output_weight,
        output_bias,
        first_gain,
        first_shift,
        widen_weight,
        widen_bias,
        shrink_weight,
        narrow_bias,
        second_gain,
        second_shift,
    )
    depth = triple_weight.shape[0]
    current = activations
    stored = []
    kept_list = []
    final = None
    for layer_params in range(depth):
        stored.append(current)
        result, kept = layer_forward(current, lengths, params, layer_params)
        kept_list.append(kept)
        final = result
        current = result.astype(jnp.bfloat16)
    outgrad = cotangent.astype(jnp.float32)
    collected = [None] * depth
    for layer_params in reversed(range(depth)):
        replayed, kept = layer_forward(stored[layer_params], lengths, params, layer_params)
        outgrad, layer_param_gradients = layer_backward(outgrad, params, layer_params, kept)
        collected[layer_params] = layer_param_gradients
    stacked = [
        jnp.stack([collected[layer_params][member] for layer_params in range(depth)])
        for member in range(12)
    ]
    group_totals = lax.psum(
        (
            stacked[0],
            stacked[1],
            stacked[6],
            stacked[7],
            stacked[8],
            stacked[9],
            stacked[10],
            stacked[11],
        ),
        "dp",
    )
    shared_totals = lax.psum((stacked[2], stacked[3], stacked[4], stacked[5]), ("dp", "grp"))
    return (
        final.astype(jnp.bfloat16),
        outgrad,
        group_totals[0],
        group_totals[1],
        shared_totals[0],
        shared_totals[1],
        shared_totals[2],
        shared_totals[3],
        group_totals[2],
        group_totals[3],
        group_totals[4],
        group_totals[5],
        group_totals[6],
        group_totals[7],
    )


def solution(mesh):
    in_specs = (
        P("dp", None, "grp"),
        P("dp", None, "grp"),
        P("dp"),
        P(None, "grp", None, None),
        P(None, None, "grp"),
        P(),
        P(),
        P(),
        P(),
        P(None, "grp", None, None),
        P(None, "grp"),
        P(None, "grp", None, None),
        P(None, "grp"),
        P(None, "grp"),
        P(None, "grp"),
    )
    out_specs = (
        P("dp", None, "grp"),
        P("dp", None, "grp"),
        P(None, "grp", None, None),
        P(None, None, "grp"),
        P(),
        P(),
        P(),
        P(),
        P(None, "grp", None, None),
        P(None, "grp"),
        P(None, "grp", None, None),
        P(None, "grp"),
        P(None, "grp"),
        P(None, "grp"),
    )
    return jax.shard_map(shards, mesh=mesh, in_specs=in_specs, out_specs=out_specs, check_vma=False)
```

profile of v0, /device:TPU:0, one launch (start us, length us, event | category | flops | bytes accessed | tf_op | source)
XLA Modules:
  0.0 857.9 jit_solution(8457950099970390052)
XLA Ops:
  31.4 6.9 all-to-all-done.3
  45.1 9.1 %all-to-all-done.2 = bf16[4,512,192]{1,2,0:T(8,128)(2,1)} async-done(((bf16[4,512,192]{1,2,0:T(8,128)(2,1)}), bf16[4,512,192]{1,2,0:T(8,128)(2,1)}, u32[]{:S(2)}, u32[]{:S(2)}) %all-to-all-start.2) | async-done | bytes 786464 | tf_op jit(solution)/shard_map/all_to_all | solution.py:134
  57.7 10.6 %fusion.129 = (f32[12,512]{1,0:T(8,128)S(1)}, f32[12,512,512]{1,2,0:T(8,128)}) fusion(pred[512]{0:T(512)(128)(4,1)S(1)} %iota_compare_fusion, bf16[512,12,64]{0,2,1:T(8,128)(2,1)} %bitcast.12, bf16[512,12,64]{0,2,1:T(8,128)(2,1)S(1)} %bitcast.431), kind=kOutput, calls=%fused_computation.281 | convolution fusion | flops 415236608 | bytes 14180864 | tf_op jit(solution)/shard_map/while/body/eval_jaxpr/sub | solution.py:42
  91.6 10.4 %all-to-all-done.4 = bf16[4,2,49152]{2,1,0:T(2,128)(2,1)S(1)} async-done(((bf16[4,2,49152]{2,1,0:T(2,128)(2,1)}), bf16[4,2,49152]{2,1,0:T(2,128)(2,1)S(1)}, u32[]{:S(2)}, u32[]{:S(2)}) %all-to-all-start.4) | async-done | bytes 786464 | tf_op jit(solution)/shard_map/all_to_all | solution.py:157
  103.8 15.9 %fusion.6 = (bf16[2048,768]{1,0:T(8,128)(2,1)S(1)}, f32[2048,768]{1,0:T(8,128)}) fusion(f32[768]{0:T(1024)S(1)} %get-tuple-element.241, bf16[2048,192]{0,1:T(8,128)(2,1)S(1)} %bitcast.493, bf16[2,1,192,768]{3,2,1,0:T(8,128)(2,1)S(1)} %copy-done.66), kind=kOutput, calls=%fused_computation.18 | convolution fusion | flops 707788800 | bytes 10522624 | tf_op jit(solution)/shard_map/dot_general | solution.py:160
  121.4 10.1 %all-reduce.6 = (f32[2048]{0:T(1024)S(1)}, f32[2048]{0:T(1024)S(1)}) all-reduce(f32[2048]{0:T(1024)S(1)} %get-tuple-element.233, f32[2048]{0:T(1024)S(1)} %get-tuple-element.232), channel_id=1, replica_groups=mesh['dp'=8,'grp'=4] {'grp'}, use_global_device_ids=true, to_apply=%region_7.8 | all-reduce | flops 4096 | bytes 32768 | tf_op jit(solution)/shard_map/psum | solution.py:171
  142.1 6.6 all-to-all-done.5
  155.4 8.5 all-to-all-done.8
  171.0 8.9 %all-to-all-done.7 = bf16[4,512,192]{1,2,0:T(8,128)(2,1)} async-done(((bf16[4,512,192]{1,2,0:T(8,128)(2,1)}), bf16[4,512,192]{1,2,0:T(8,128)(2,1)}, u32[]{:S(2)}, u32[]{:S(2)}) %all-to-all-start.7) | async-done | bytes 786464 | tf_op jit(solution)/shard_map/all_to_all | solution.py:134
  183.4 10.5 %fusion.131 = (f32[12,512]{1,0:T(8,128)S(1)}, f32[12,512,512]{1,2,0:T(8,128)}) fusion(pred[512]{0:T(512)(128)(4,1)S(1)} %iota_compare_fusion, bf16[512,12,64]{0,2,1:T(8,128)(2,1)} %bitcast.37, bf16[512,12,64]{0,2,1:T(8,128)(2,1)S(1)} %bitcast.433), kind=kOutput, calls=%fused_computation.283 | convolution fusion | flops 415236608 | bytes 14180864 | tf_op jit(solution)/shard_map/while/body/eval_jaxpr/sub | solution.py:42
  207.6 6.3 reduce.29
  221.9 10.4 %all-to-all-done.9 = bf16[4,2,49152]{2,1,0:T(2,128)(2,1)} async-done(((bf16[4,2,49152]{2,1,0:T(2,128)(2,1)}), bf16[4,2,49152]{2,1,0:T(2,128)(2,1)}, u32[]{:S(2)}, u32[]{:S(2)}) %all-to-all-start.9) | async-done | bytes 786464 | tf_op jit(solution)/shard_map/all_to_all | solution.py:157
  238.5 15.8 %fusion.9 = (bf16[2048,768]{1,0:T(8,128)(2,1)S(1)}, f32[2048,768]{1,0:T(8,128)}) fusion(f32[768]{0:T(1024)S(1)} %get-tuple-element.240, bf16[2048,192]{0,1:T(8,128)(2,1)S(1)} %bitcast.497, bf16[2,1,192,768]{3,2,1,0:T(8,128)(2,1)S(1)} %copy-done.67), kind=kOutput, calls=%fused_computation.21 | convolution fusion | flops 707788800 | bytes 10522624 | tf_op jit(solution)/shard_map/dot_general | solution.py:160
  256.7 10.3 %all-reduce.5 = (f32[2048]{0:T(1024)S(1)}, f32[2048]{0:T(1024)S(1)}) all-reduce(f32[2048]{0:T(1024)S(1)} %get-tuple-element.231, f32[2048]{0:T(1024)S(1)} %get-tuple-element.230), channel_id=1, replica_groups=mesh['dp'=8,'grp'=4] {'grp'}, use_global_device_ids=true, to_apply=%region_15.16 | all-reduce | flops 4096 | bytes 32768 | tf_op jit(solution)/shard_map/psum | solution.py:171
  269.4 10.3 %all-reduce.4 = (f32[2048]{0:T(1024)S(1)}, f32[2048]{0:T(1024)S(1)}) all-reduce(f32[2048]{0:T(1024)S(1)} %get-tuple-element.223, f32[2048]{0:T(1024)S(1)} %bitcast.523), channel_id=1, replica_groups=mesh['dp'=8,'grp'=4] {'grp'}, use_global_device_ids=true, to_apply=%region_19.20 | all-reduce | flops 4096 | bytes 32768 | tf_op jit(solution)/shard_map/psum | solution.py:237
  283.9 6.3 convert_reduce_fusion
  297.1 11.6 %all-to-all-done.10 = bf16[4,512,192]{1,2,0:T(8,128)(2,1)} async-done(((bf16[4,512,192]{1,2,0:T(8,128)(2,1)}), bf16[4,512,192]{1,2,0:T(8,128)(2,1)}, u32[]{:S(2)}, u32[]{:S(2)}) %all-to-all-start.10) | async-done | bytes 786464 | tf_op jit(solution)/shard_map/all_to_all | solution.py:253
  322.3 6.9 fusion.70
  342.8 11.6 %multiply_reduce_fusion.1 = (f32[12,512]{1,0:T(8,128)S(1)}, f32[12,512,512]{1,2,0:T(8,128)}) fusion(f32[12,512,512]{1,2,0:T(8,128)} %get-tuple-element.302, f32[12,512]{1,0:T(8,128)S(1)} %get-tuple-element.301, bf16[512,12,64]{0,2,1:T(8,128)(2,1)} %bitcast.513, bf16[512,12,64]{0,2,1:T(8,128)(2,1)} %bitcast.510), kind=kOutput, calls=%fused_computation.5 | convolution fusion | flops 412084224 | bytes 26787840 | tf_op jit(solution)/shard_map/while/body/eval_jaxpr/qhd,khd->hqk/dot_general | solution.py:61
  357.3 6.4 reduce.30
  369.7 9.6 %multiply_convert_fusion.1 = bf16[12,512,512]{1,2,0:T(8,128)(2,1)S(1)} fusion(f32[12,512,512]{1,2,0:T(8,128)} %get-tuple-element.309, f32[12,512]{1,0:T(8,128)S(1)} %get-tuple-element.308, f32[12,512,512]{1,2,0:T(8,128)} %get-tuple-element.302, f32[12,512]{1,0:T(8,128)S(1)} %get-tuple-element.301), kind=kLoop, calls=%fused_computation.4 | loop fusion | flops 12582912 | bytes 31506432 | tf_op jit(solution)/shard_map/while/body/eval_jaxpr/convert_element_type | solution.py:65
  385.4 6.5 reduce.32
  404.0 6.4 reduce.31
  440.9 11.9 %all-reduce.3 = (f32[2048]{0:T(1024)S(1)}, f32[2048]{0:T(1024)S(1)}) all-reduce(f32[2048]{0:T(1024)S(1)} %get-tuple-element.221, f32[2048]{0:T(1024)S(1)} %get-tuple-element.228), channel_id=1, replica_groups=mesh['dp'=8,'grp'=4] {'grp'}, use_global_device_ids=true, to_apply=%region_26.27 | all-reduce | flops 4096 | bytes 32768 | tf_op jit(solution)/shard_map/psum | solution.py:237
  489.2 6.7 fusion.64
  495.9 8.9 %multiply_reduce_fusion = (f32[12,512]{1,0:T(8,128)S(1)}, f32[12,512,512]{1,2,0:T(8,128)}) fusion(f32[12,512,512]{1,2,0:T(8,128)} %get-tuple-element.295, f32[12,512]{1,0:T(8,128)S(1)} %copy-done.81, bf16[512,12,64]{0,2,1:T(8,128)(2,1)S(1)} %bitcast.515, bf16[512,12,64]{0,2,1:T(8,128)(2,1)S(1)} %bitcast.508), kind=kOutput, calls=%fused_computation.3 | convolution fusion | flops 412084224 | bytes 26787840 | tf_op jit(solution)/shard_map/while/body/eval_jaxpr/qhd,khd->hqk/dot_general | solution.py:61
  517.2 9.6 %multiply_convert_fusion = bf16[12,512,512]{1,2,0:T(8,128)(2,1)S(1)} fusion(f32[12,512,512]{1,2,0:T(8,128)} %get-tuple-element.312, f32[12,512]{1,0:T(8,128)S(1)} %get-tuple-element.311, f32[12,512,512]{1,2,0:T(8,128)} %get-tuple-element.295, f32[12,512]{1,0:T(8,128)S(1)} %copy-done.81), kind=kLoop, calls=%fused_computation.2 | loop fusion | flops 12582912 | bytes 31506432 | tf_op jit(solution)/shard_map/while/body/eval_jaxpr/convert_element_type | solution.py:65
  558.1 7.5 reduce.35
  601.3 6.3 reduce.34
  614.4 47.1 %all-reduce = (f32[2,768]{1,0:T(2,128)}, f32[2,768]{1,0:T(2,128)}, f32[2,768]{1,0:T(2,128)}) all-reduce(f32[2,768]{1,0:T(2,128)S(1)} %pad_maximum_fusion.4, f32[2,768]{1,0:T(2,128)S(1)} %pad_maximum_fusion.5, f32[2,768]{1,0:T(2,128)S(1)} %pad_maximum_fusion.6), channel_id=1, replica_groups=mesh['dp'=8,'grp'=4] {'dp','grp'}, use_global_device_ids=true, to_apply=%region_39.40 | all-reduce | flops 4608 | bytes 36864 | tf_op jit(solution)/shard_map/psum | solution.py:384
  668.6 37.8 %all-reduce.1 = (f32[2,2,192]{2,1,0:T(2,128)}, f32[2,768]{1,0:T(2,128)}, f32[2,192]{1,0:T(2,128)}, f32[2,192]{1,0:T(2,128)}, f32[2,192]{1,0:T(2,128)}) all-reduce(f32[2,2,192]{2,1,0:T(2,128)S(1)} %pad_maximum_fusion.8, f32[2,768]{1,0:T(2,128)S(1)} %pad_maximum_fusion.7, ...), channel_id=1, replica_groups=mesh['dp'=8,'grp'=4] {'dp'}, use_global_device_ids=true, to_apply=%region_35.36 | all-reduce | flops 3456 | bytes 27648 | tf_op jit(solution)/shard_map/psum | solution.py:371
  706.3 134.4 %all-reduce.12.cloned.1.call-done = (f32[2,1,192,576]{3,2,1,0:T(8,128)}, f32[2,1,192,768]{3,2,1,0:T(8,128)}, f32[2,1,768,192]{2,3,1,0:T(8,128)}) async-done(((f32[2,1,192,576]{3,2,1,0:T(8,128)}, f32[2,1,192,768]{3,2,1,0:T(8,128)}, f32[2,1,768,192]{2,3,1,0:T(8,128)}), (f32[2,1,192,576]{3,2,1,0:T(8,128)}, f32[2,1,192,768]{3,2,1,0:T(8,128)}, f32[2,1,768,192]{2,3,1,0:T(8,128)})) %all-reduce.12.cloned.1.call-update) | async-done | bytes 3244048 | tf_op jit(solution)/shard_map/psum | solution.py:371
  (458 shorter events, 355.2 us)
Async XLA Ops:
  7.2 16.0 %all-to-all-start = ((bf16[4,512,192]{1,2,0:T(8,128)(2,1)}), bf16[4,512,192]{1,2,0:T(8,128)(2,1)S(1)}, u32[]{:S(2)}, u32[]{:S(2)}) async-start(bf16[4,512,192]{1,2,0:T(8,128)(2,1)} %param.15), calls=%async_computation | async-start | bytes 1572864 | tf_op jit(solution)/shard_map/all_to_all | solution.py:137
  23.2 15.1 %all-to-all-start.3 = ((bf16[4,512,192]{1,2,0:T(8,128)(2,1)}), bf16[4,512,192]{1,2,0:T(8,128)(2,1)S(1)}, u32[]{:S(2)}, u32[]{:S(2)}) async-start(bf16[4,512,192]{1,2,0:T(8,128)(2,1)} %bitcast.407), calls=%async_computation.3 | async-start | bytes 1572864 | tf_op jit(solution)/shard_map/all_to_all | solution.py:135
  38.3 19.4 %copy-start.32 = (bf16[4,512,192]{1,2,0:T(8,128)(2,1)}, bf16[4,512,192]{1,2,0:T(8,128)(2,1)S(1)}, u32[]{:S(2)}) copy-start(bf16[4,512,192]{1,2,0:T(8,128)(2,1)S(1)} %all-to-all-done.3) | copy-start | bytes 2359300
  38.3 15.9 %all-to-all-start.2 = ((bf16[4,512,192]{1,2,0:T(8,128)(2,1)}), bf16[4,512,192]{1,2,0:T(8,128)(2,1)}, u32[]{:S(2)}, u32[]{:S(2)}) async-start(bf16[4,512,192]{1,2,0:T(8,128)(2,1)} %bitcast.408), calls=%async_computation.2 | async-start | bytes 1572864 | tf_op jit(solution)/shard_map/all_to_all | solution.py:134
  43.3 33.6 %copy-start.74 = (f32[768]{0:T(1024)}, f32[768]{0:T(1024)S(1)}, u32[]{:S(2)}) copy-start(f32[768]{0:T(1024)S(1)} %get-tuple-element.317) | copy-start | bytes 9220
  54.2 15.1 %all-to-all-start.1 = ((bf16[4,512,192]{1,2,0:T(8,128)(2,1)}), bf16[4,512,192]{1,2,0:T(8,128)(2,1)S(1)}, u32[]{:S(2)}, u32[]{:S(2)}) async-start(bf16[4,512,192]{1,2,0:T(8,128)(2,1)} %bitcast.409), calls=%async_computation.1 | async-start | bytes 1572864 | tf_op jit(solution)/shard_map/all_to_all | solution.py:136
  86.8 15.1 %all-to-all-start.4 = ((bf16[4,2,49152]{2,1,0:T(2,128)(2,1)}), bf16[4,2,49152]{2,1,0:T(2,128)(2,1)S(1)}, u32[]{:S(2)}, u32[]{:S(2)}) async-start(bf16[4,2,49152]{2,1,0:T(2,128)(2,1)} %reshape.507), calls=%async_computation.4 | async-start | bytes 1572864 | tf_op jit(solution)/shard_map/all_to_all | solution.py:157
  91.0 40.6 %copy-start.82 = (f32[1,192]{1,0:T(1,128)}, f32[1,192]{1,0:T(1,128)S(1)}, u32[]{:S(2)}) copy-start(f32[1,192]{1,0:T(1,128)S(1)} %get-tuple-element.289) | copy-start | bytes 2308
  103.7 15.9 %copy-start.47 = (bf16[24,8,4,512]{3,1,2,0:T(8,128)(2,1)}, bf16[24,8,4,512]{3,1,2,0:T(8,128)(2,1)S(1)}, u32[]{:S(2)}) copy-start(bf16[24,8,4,512]{3,1,2,0:T(8,128)(2,1)S(1)} %copy.218) | copy-start | bytes 2359300
  103.8 15.9 %copy-start.107 = (bf16[2,1,768,192]{2,3,1,0:T(8,128)(2,1)S(1)}, bf16[2,1,768,192]{2,3,1,0:T(8,128)(2,1)}, u32[]{:S(2)}) copy-start(bf16[2,1,768,192]{2,3,1,0:T(8,128)(2,1)} %param.26) | copy-start | bytes 1769476
  121.4 17.4 %copy-start.16 = (f32[2048,192]{0,1:T(8,128)}, f32[2048,192]{0,1:T(8,128)S(1)}, u32[]{:S(2)}) copy-start(f32[2048,192]{0,1:T(8,128)S(1)} %get-tuple-element.300) | copy-start | bytes 4718596
  133.5 15.1 %all-to-all-start.5 = ((bf16[4,512,192]{1,2,0:T(8,128)(2,1)}), bf16[4,512,192]{1,2,0:T(8,128)(2,1)S(1)}, u32[]{:S(2)}, u32[]{:S(2)}) async-start(bf16[4,512,192]{1,2,0:T(8,128)(2,1)} %bitcast.406), calls=%async_computation.5 | async-start | bytes 1572864 | tf_op jit(solution)/shard_map/all_to_all | solution.py:137
  148.7 15.3 %all-to-all-start.8 = ((bf16[4,512,192]{1,2,0:T(8,128)(2,1)}), bf16[4,512,192]{1,2,0:T(8,128)(2,1)S(1)}, u32[]{:S(2)}, u32[]{:S(2)}) async-start(bf16[4,512,192]{1,2,0:T(8,128)(2,1)} %bitcast.403), calls=%async_computation.8 | async-start | bytes 1572864 | tf_op jit(solution)/shard_map/all_to_all | solution.py:135
  164.0 19.4 %copy-start.34 = (bf16[4,512,192]{1,2,0:T(8,128)(2,1)}, bf16[4,512,192]{1,2,0:T(8,128)(2,1)S(1)}, u32[]{:S(2)}) copy-start(bf16[4,512,192]{1,2,0:T(8,128)(2,1)S(1)} %all-to-all-done.8) | copy-start | bytes 2359300
  164.0 15.9 %all-to-all-start.7 = ((bf16[4,512,192]{1,2,0:T(8,128)(2,1)}), bf16[4,512,192]{1,2,0:T(8,128)(2,1)}, u32[]{:S(2)}, u32[]{:S(2)}) async-start(bf16[4,512,192]{1,2,0:T(8,128)(2,1)} %bitcast.404), calls=%async_computation.7 | async-start | bytes 1572864 | tf_op jit(solution)/shard_map/all_to_all | solution.py:134
  179.9 15.1 %all-to-all-start.6 = ((bf16[4,512,192]{1,2,0:T(8,128)(2,1)}), bf16[4,512,192]{1,2,0:T(8,128)(2,1)S(1)}, u32[]{:S(2)}, u32[]{:S(2)}) async-start(bf16[4,512,192]{1,2,0:T(8,128)(2,1)} %bitcast.405), calls=%async_computation.6 | async-start | bytes 1572864 | tf_op jit(solution)/shard_map/all_to_all | solution.py:136
  216.3 15.9 %all-to-all-start.9 = ((bf16[4,2,49152]{2,1,0:T(2,128)(2,1)}), bf16[4,2,49152]{2,1,0:T(2,128)(2,1)}, u32[]{:S(2)}, u32[]{:S(2)}) async-start(bf16[4,2,49152]{2,1,0:T(2,128)(2,1)} %reshape.509), calls=%async_computation.9 | async-start | bytes 1572864 | tf_op jit(solution)/shard_map/all_to_all | solution.py:157
  221.9 45.1 %copy-start.14 = (f32[4,24,8,512]{3,2,0,1:T(8,128)}, f32[4,24,8,512]{3,2,0,1:T(8,128)S(1)}, u32[]{:S(2)}) copy-start(f32[4,24,8,512]{3,2,0,1:T(8,128)S(1)} %copy.217) | copy-start | bytes 4718596
  238.4 15.9 %copy-start.48 = (bf16[24,8,4,512]{3,1,2,0:T(8,128)(2,1)}, bf16[24,8,4,512]{3,1,2,0:T(8,128)(2,1)S(1)}, u32[]{:S(2)}) copy-start(bf16[24,8,4,512]{3,1,2,0:T(8,128)(2,1)S(1)} %copy.219) | copy-start | bytes 2359300
  256.7 23.0 %copy-start.98 = (f32[1,192]{1,0:T(1,128)S(1)}, f32[1,192]{1,0:T(1,128)}, u32[]{:S(2)}) copy-start(f32[1,192]{1,0:T(1,128)} %get-tuple-element.290) | copy-start | bytes 2308
  292.8 15.9 %all-to-all-start.10 = ((bf16[4,512,192]{1,2,0:T(8,128)(2,1)}), bf16[4,512,192]{1,2,0:T(8,128)(2,1)}, u32[]{:S(2)}, u32[]{:S(2)}) async-start(bf16[4,512,192]{1,2,0:T(8,128)(2,1)} %bitcast.474), calls=%async_computation.10 | async-start | bytes 1572864 | tf_op jit(solution)/shard_map/all_to_all | solution.py:253
  339.1 26.0 %all-to-all-start.13 = ((bf16[4,2,49152]{2,1,0:T(2,128)(2,1)}), bf16[4,2,49152]{2,1,0:T(2,128)(2,1)S(1)}, u32[]{:S(2)}, u32[]{:S(2)}) async-start(bf16[4,2,49152]{2,1,0:T(2,128)(2,1)} %reshape.517), calls=%async_computation.13 | async-start | bytes 1572864 | tf_op jit(solution)/shard_map/all_to_all | solution.py:281
  365.1 28.2 %all-to-all-start.14 = ((bf16[4,2,49152]{2,1,0:T(2,128)(2,1)}), bf16[4,2,49152]{2,1,0:T(2,128)(2,1)}, u32[]{:S(2)}, u32[]{:S(2)}) async-start(bf16[4,2,49152]{2,1,0:T(2,128)(2,1)} %reshape.511), calls=%async_computation.14 | async-start | bytes 1572864 | tf_op jit(solution)/shard_map/all_to_all | solution.py:282
  393.3 18.5 %all-to-all-start.12 = ((bf16[4,2,49152]{2,1,0:T(2,128)(2,1)}), bf16[4,2,49152]{2,1,0:T(2,128)(2,1)}, u32[]{:S(2)}, u32[]{:S(2)}) async-start(bf16[4,2,49152]{2,1,0:T(2,128)(2,1)} %reshape.515), calls=%async_computation.12 | async-start | bytes 1572864 | tf_op jit(solution)/shard_map/all_to_all | solution.py:280
  411.8 22.0 %all-to-all-start.11 = ((bf16[4,2,49152]{2,1,0:T(2,128)(2,1)}), bf16[4,2,49152]{2,1,0:T(2,128)(2,1)}, u32[]{:S(2)}, u32[]{:S(2)}) async-start(bf16[4,2,49152]{2,1,0:T(2,128)(2,1)} %reshape.513), calls=%async_computation.11 | async-start | bytes 1572864 | tf_op jit(solution)/shard_map/all_to_all | solution.py:279
  463.8 16.3 %all-to-all-start.15 = ((bf16[4,512,192]{1,2,0:T(8,128)(2,1)}), bf16[4,512,192]{1,2,0:T(8,128)(2,1)}, u32[]{:S(2)}, u32[]{:S(2)}) async-start(bf16[4,512,192]{1,2,0:T(8,128)(2,1)} %bitcast.473), calls=%async_computation.15 | async-start | bytes 1572864 | tf_op jit(solution)/shard_map/all_to_all | solution.py:253
  512.8 29.3 %all-to-all-start.18 = ((bf16[4,2,49152]{2,1,0:T(2,128)(2,1)}), bf16[4,2,49152]{2,1,0:T(2,128)(2,1)}, u32[]{:S(2)}, u32[]{:S(2)}) async-start(bf16[4,2,49152]{2,1,0:T(2,128)(2,1)} %reshape.525), calls=%async_computation.18 | async-start | bytes 1572864 | tf_op jit(solution)/shard_map/all_to_all | solution.py:281
  542.1 25.9 %all-to-all-start.17 = ((bf16[4,2,49152]{2,1,0:T(2,128)(2,1)}), bf16[4,2,49152]{2,1,0:T(2,128)(2,1)}, u32[]{:S(2)}, u32[]{:S(2)}) async-start(bf16[4,2,49152]{2,1,0:T(2,128)(2,1)} %reshape.523), calls=%async_computation.17 | async-start | bytes 1572864 | tf_op jit(solution)/shard_map/all_to_all | solution.py:280
  546.3 160.1 %all-reduce.10.cloned.1.call-start = ((), (), s32[]{:S(2)}) async-start(), calls=%async_computation.20 | async-start | bytes 9437184 | tf_op jit(solution)/shard_map/psum | solution.py:384
  568.0 19.9 %all-to-all-start.16 = ((bf16[4,2,49152]{2,1,0:T(2,128)(2,1)}), bf16[4,2,49152]{2,1,0:T(2,128)(2,1)}, u32[]{:S(2)}, u32[]{:S(2)}) async-start(bf16[4,2,49152]{2,1,0:T(2,128)(2,1)} %reshape.521), calls=%async_computation.16 | async-start | bytes 1572864 | tf_op jit(solution)/shard_map/all_to_all | solution.py:279
  572.2 268.6 %all-reduce.12.cloned.1.call-start = ((), (), s32[]{:S(2)}) async-start(), calls=%async_computation.21 | async-start | bytes 6684672 | tf_op jit(solution)/shard_map/psum | solution.py:371
  610.0 51.5 %all-to-all-start.19 = ((bf16[4,2,49152]{2,1,0:T(2,128)(2,1)}), bf16[4,2,49152]{2,1,0:T(2,128)(2,1)}, u32[]{:S(2)}, u32[]{:S(2)}) async-start(bf16[4,2,49152]{2,1,0:T(2,128)(2,1)} %reshape.519), calls=%async_computation.19 | async-start | bytes 1572864 | tf_op jit(solution)/shard_map/all_to_all | solution.py:282
  (101 other events, 549.0 us)
Sparse Core Ops, SparseCore 0:
  553.3 147.5 all-reduce.9
  706.6 134.1 all-reduce.11
where the time goes:
time: 869 us; the launch traced here: 858 us
  waiting for transfers between devices  219 us (25%)
  matrix products  162 us (19%)
  local copies, waits for them, and re-layouts  131 us (15%)
  blocking collectives  127 us (15%)
  other arithmetic  121 us (14%)
  starting transfers between devices  81.2 us (9%)
  between operations  16.6 us (2%)
    psum x1, waiting for transfers between devices, shards(): lax.psum((stacked[0], stacked[1], stacked[6], stacked[7], stacked[8], sta...  134 us
    unnamed x270, local copies, waits for them, and re-layouts  76.3 us
    unnamed x11, other arithmetic  62.1 us
    psum x1, blocking collectives, shards(): lax.psum((stacked[2], stacked[3], stacked[4], stacked[5]), ('dp', 'grp'))  47.1 us
    psum x1, blocking collectives, shards(): lax.psum((stacked[0], stacked[1], stacked[6], stacked[7], stacked[8], sta...  37.8 us
    dot_general x2, matrix products, layer_forward(): jnp.dot(group_rows, widen_weight[layer_params, 0], preferred_element_type...  31.7 us
    psum x2, blocking collectives, layer_backward(): total_sum, total_cross = lax.psum((part_sum, part_cross), 'grp')  22.2 us
    sub x2, matrix products, single(): expon = jnp.exp(scores - highest)  21.1 us
  transfers between devices with their start and end apart: 22, of which 13 were waited for; matrix products, arithmetic and copies ran while one was open for 25% of the time, Pallas kernels for 0%

commit v1 on v0

--- a/solution.py
+++ b/solution.py
@@ -7,6 +7,11 @@
 HEAD = 64
 EPSILON = 1e-05
 MASKED = -1e30
+
+
+def axis_by_axis(x, first, second):
+    partial = lax.psum(x, first)
+    return lax.psum(partial, second)
 
 
 def contract_rows(left, right):
@@ -381,7 +386,7 @@
         ),
         "dp",
     )
-    shared_totals = lax.psum((stacked[2], stacked[3], stacked[4], stacked[5]), ("dp", "grp"))
+    shared_totals = axis_by_axis((stacked[2], stacked[3], stacked[4], stacked[5]), "grp", "dp")
     return (
         final.astype(jnp.bfloat16),
         outgrad,

time: 869 us -> 953 us (1.097)
  waiting for transfers between devices: 219 us -> 329 us
  blocking collectives: 127 us -> 101 us
    psum x1, waiting for transfers between devices: 0.01 us -> 55.5 us  [axis_by_axis(): partial = lax.psum(x, first)]
    psum x1, waiting for transfers between devices: 134 us -> 184 us  [shards(): lax.psum((stacked[0], stacked[1], stacked[6], stacked[7], stacked[8], sta...]
    psum x1, blocking collectives: 47.1 us -> 17.8 us  [axis_by_axis(): partial = lax.psum(x, first)]
  transfers between devices with their start and end apart: 22 -> 22, of which waited for: 13 -> 15; matrix products, arithmetic and copies ran while one was open for 25% -> 23% of each run, Pallas kernels for 0% -> 0%
where the time goes in v1:
time: 953 us; the launch traced here: 943 us
  waiting for transfers between devices  329 us (35%)
  matrix products  162 us (17%)
  local copies, waits for them, and re-layouts  132 us (14%)
  other arithmetic  121 us (13%)
  blocking collectives  101 us (11%)
  starting transfers between devices  81.2 us (9%)
  between operations  16.6 us (2%)
    psum x1, waiting for transfers between devices, shards(): lax.psum((stacked[0], stacked[1], stacked[6], stacked[7], stacked[8], sta...  184 us
    unnamed x270, local copies, waits for them, and re-layouts  77.1 us
    unnamed x11, other arithmetic  62.7 us
    psum x1, waiting for transfers between devices, axis_by_axis(): partial = lax.psum(x, first)  55.5 us
    psum x1, blocking collectives, shards(): lax.psum((stacked[0], stacked[1], stacked[6], stacked[7], stacked[8], sta...  40.7 us
    dot_general x2, matrix products, layer_forward(): jnp.dot(group_rows, widen_weight[layer_params, 0], preferred_element_type...  31.7 us
    psum x2, blocking collectives, layer_backward(): total_sum, total_cross = lax.psum((part_sum, part_cross), 'grp')  22.2 us
    sub x2, matrix products, single(): expon = jnp.exp(scores - highest)  21.1 us
  transfers between devices with their start and end apart: 22, of which 15 were waited for; matrix products, arithmetic and copies ran while one was open for 23% of the time, Pallas kernels for 0%

profile of v1, /device:TPU:0, one launch (start us, length us, event | category | flops | bytes accessed | tf_op | source)
XLA Modules:
  0.0 942.7 jit_solution(5546048368971954384)
XLA Ops:
  31.4 6.9 all-to-all-done.3
  45.1 9.1 all-to-all-done.2
  57.7 10.6 %fusion.129 = (f32[12,512]{1,0:T(8,128)S(1)}, f32[12,512,512]{1,2,0:T(8,128)}) fusion(pred[512]{0:T(512)(128)(4,1)S(1)} %iota_compare_fusion, bf16[512,12,64]{0,2,1:T(8,128)(2,1)} %bitcast.12, bf16[512,12,64]{0,2,1:T(8,128)(2,1)S(1)} %bitcast.431), kind=kOutput, calls=%fused_computation.281 | convolution fusion | flops 415236608 | bytes 14180864 | tf_op jit(solution)/shard_map/while/body/eval_jaxpr/sub | solution.py:47
  91.6 10.4 %all-to-all-done.4 = bf16[4,2,49152]{2,1,0:T(2,128)(2,1)S(1)} async-done(((bf16[4,2,49152]{2,1,0:T(2,128)(2,1)}), bf16[4,2,49152]{2,1,0:T(2,128)(2,1)S(1)}, u32[]{:S(2)}, u32[]{:S(2)}) %all-to-all-start.4) | async-done | bytes 786464 | tf_op jit(solution)/shard_map/all_to_all | solution.py:162
  103.8 15.9 %fusion.6 = (bf16[2048,768]{1,0:T(8,128)(2,1)S(1)}, f32[2048,768]{1,0:T(8,128)}) fusion(f32[768]{0:T(1024)S(1)} %get-tuple-element.241, bf16[2048,192]{0,1:T(8,128)(2,1)S(1)} %bitcast.493, bf16[2,1,192,768]{3,2,1,0:T(8,128)(2,1)S(1)} %copy-done.66), kind=kOutput, calls=%fused_computation.18 | convolution fusion | flops 707788800 | bytes 10522624 | tf_op jit(solution)/shard_map/dot_general | solution.py:165
  121.4 10.1 %all-reduce.6 = (f32[2048]{0:T(1024)S(1)}, f32[2048]{0:T(1024)S(1)}) all-reduce(f32[2048]{0:T(1024)S(1)} %get-tuple-element.233, f32[2048]{0:T(1024)S(1)} %get-tuple-element.232), channel_id=1, replica_groups=mesh['dp'=8,'grp'=4] {'grp'}, use_global_device_ids=true, to_apply=%region_7.8 | all-reduce | flops 4096 | bytes 32768 | tf_op jit(solution)/shard_map/psum | solution.py:176
  142.1 6.6 all-to-all-done.5
  155.5 8.5 all-to-all-done.8
  171.0 8.9 all-to-all-done.7
  183.4 10.5 %fusion.131 = (f32[12,512]{1,0:T(8,128)S(1)}, f32[12,512,512]{1,2,0:T(8,128)}) fusion(pred[512]{0:T(512)(128)(4,1)S(1)} %iota_compare_fusion, bf16[512,12,64]{0,2,1:T(8,128)(2,1)} %bitcast.37, bf16[512,12,64]{0,2,1:T(8,128)(2,1)S(1)} %bitcast.433), kind=kOutput, calls=%fused_computation.283 | convolution fusion | flops 415236608 | bytes 14180864 | tf_op jit(solution)/shard_map/while/body/eval_jaxpr/sub | solution.py:47
  207.6 6.3 reduce.29
  221.9 10.4 %all-to-all-done.9 = bf16[4,2,49152]{2,1,0:T(2,128)(2,1)} async-done(((bf16[4,2,49152]{2,1,0:T(2,128)(2,1)}), bf16[4,2,49152]{2,1,0:T(2,128)(2,1)}, u32[]{:S(2)}, u32[]{:S(2)}) %all-to-all-start.9) | async-done | bytes 786464 | tf_op jit(solution)/shard_map/all_to_all | solution.py:162
  238.5 15.8 %fusion.9 = (bf16[2048,768]{1,0:T(8,128)(2,1)S(1)}, f32[2048,768]{1,0:T(8,128)}) fusion(f32[768]{0:T(1024)S(1)} %get-tuple-element.240, bf16[2048,192]{0,1:T(8,128)(2,1)S(1)} %bitcast.497, bf16[2,1,192,768]{3,2,1,0:T(8,128)(2,1)S(1)} %copy-done.67), kind=kOutput, calls=%fused_computation.21 | convolution fusion | flops 707788800 | bytes 10522624 | tf_op jit(solution)/shard_map/dot_general | solution.py:165
  256.7 10.3 %all-reduce.5 = (f32[2048]{0:T(1024)S(1)}, f32[2048]{0:T(1024)S(1)}) all-reduce(f32[2048]{0:T(1024)S(1)} %get-tuple-element.231, f32[2048]{0:T(1024)S(1)} %get-tuple-element.230), channel_id=1, replica_groups=mesh['dp'=8,'grp'=4] {'grp'}, use_global_device_ids=true, to_apply=%region_15.16 | all-reduce | flops 4096 | bytes 32768 | tf_op jit(solution)/shard_map/psum | solution.py:176
  269.4 10.3 %all-reduce.4 = (f32[2048]{0:T(1024)S(1)}, f32[2048]{0:T(1024)S(1)}) all-reduce(f32[2048]{0:T(1024)S(1)} %get-tuple-element.223, f32[2048]{0:T(1024)S(1)} %bitcast.523), channel_id=1, replica_groups=mesh['dp'=8,'grp'=4] {'grp'}, use_global_device_ids=true, to_apply=%region_19.20 | all-reduce | flops 4096 | bytes 32768 | tf_op jit(solution)/shard_map/psum | solution.py:242
  283.8 6.3 convert_reduce_fusion
  297.1 11.6 %all-to-all-done.10 = bf16[4,512,192]{1,2,0:T(8,128)(2,1)} async-done(((bf16[4,512,192]{1,2,0:T(8,128)(2,1)}), bf16[4,512,192]{1,2,0:T(8,128)(2,1)}, u32[]{:S(2)}, u32[]{:S(2)}) %all-to-all-start.10) | async-done | bytes 786464 | tf_op jit(solution)/shard_map/all_to_all | solution.py:258
  322.3 6.9 fusion.70
  342.8 11.6 %multiply_reduce_fusion.1 = (f32[12,512]{1,0:T(8,128)S(1)}, f32[12,512,512]{1,2,0:T(8,128)}) fusion(f32[12,512,512]{1,2,0:T(8,128)} %get-tuple-element.306, f32[12,512]{1,0:T(8,128)S(1)} %get-tuple-element.305, bf16[512,12,64]{0,2,1:T(8,128)(2,1)} %bitcast.513, bf16[512,12,64]{0,2,1:T(8,128)(2,1)} %bitcast.510), kind=kOutput, calls=%fused_computation.5 | convolution fusion | flops 412084224 | bytes 26787840 | tf_op jit(solution)/shard_map/while/body/eval_jaxpr/qhd,khd->hqk/dot_general | solution.py:66
  357.3 6.4 reduce.30
  369.6 9.6 %multiply_convert_fusion.1 = bf16[12,512,512]{1,2,0:T(8,128)(2,1)S(1)} fusion(f32[12,512,512]{1,2,0:T(8,128)} %get-tuple-element.313, f32[12,512]{1,0:T(8,128)S(1)} %get-tuple-element.312, f32[12,512,512]{1,2,0:T(8,128)} %get-tuple-element.306, f32[12,512]{1,0:T(8,128)S(1)} %get-tuple-element.305), kind=kLoop, calls=%fused_computation.4 | loop fusion | flops 12582912 | bytes 31506432 | tf_op jit(solution)/shard_map/while/body/eval_jaxpr/convert_element_type | solution.py:70
  385.4 6.5 reduce.32
  404.0 6.4 reduce.31
  440.9 11.9 %all-reduce.3 = (f32[2048]{0:T(1024)S(1)}, f32[2048]{0:T(1024)S(1)}) all-reduce(f32[2048]{0:T(1024)S(1)} %get-tuple-element.221, f32[2048]{0:T(1024)S(1)} %get-tuple-element.228), channel_id=1, replica_groups=mesh['dp'=8,'grp'=4] {'grp'}, use_global_device_ids=true, to_apply=%region_26.27 | all-reduce | flops 4096 | bytes 32768 | tf_op jit(solution)/shard_map/psum | solution.py:242
  489.2 6.7 fusion.64
  495.8 8.9 multiply_reduce_fusion
  517.1 9.6 %multiply_convert_fusion = bf16[12,512,512]{1,2,0:T(8,128)(2,1)S(1)} fusion(f32[12,512,512]{1,2,0:T(8,128)} %get-tuple-element.316, f32[12,512]{1,0:T(8,128)S(1)} %get-tuple-element.315, f32[12,512,512]{1,2,0:T(8,128)} %get-tuple-element.299, f32[12,512]{1,0:T(8,128)S(1)} %copy-done.81), kind=kLoop, calls=%fused_computation.2 | loop fusion | flops 12582912 | bytes 31506432 | tf_op jit(solution)/shard_map/while/body/eval_jaxpr/convert_element_type | solution.py:70
  558.1 8.0 reduce.35
  600.3 55.5 %all-reduce.10.cloned.1.call-done = f32[2,768,768]{2,1,0:T(8,128)} async-done(((f32[2,768,768]{2,1,0:T(8,128)}), f32[2,768,768]{2,1,0:T(8,128)}) %all-reduce.10.cloned.1.call-update) | async-done | bytes 4718608 | tf_op jit(solution)/shard_map/psum | solution.py:13
  675.7 17.8 %all-reduce.2 = (f32[2,768]{1,0:T(2,128)S(1)}, f32[2,768]{1,0:T(2,128)S(1)}, f32[2,768]{1,0:T(2,128)S(1)}) all-reduce(f32[2,768]{1,0:T(2,128)S(1)} %pad_maximum_fusion.4, f32[2,768]{1,0:T(2,128)S(1)} %pad_maximum_fusion.5, f32[2,768]{1,0:T(2,128)S(1)} %pad_maximum_fusion.6), channel_id=1, replica_groups=mesh['dp'=8,'grp'=4] {'grp'}, use_global_device_ids=true, to_apply=%region_40.41 | all-reduce | flops 4608 | bytes 36864 | tf_op jit(solution)/shard_map/psum | solution.py:13
  700.7 40.7 %all-reduce = (f32[2,2,192]{2,1,0:T(2,128)}, f32[2,768]{1,0:T(2,128)}, f32[2,768]{1,0:T(2,128)}, f32[2,768]{1,0:T(2,128)}, f32[2,768]{1,0:T(2,128)}, /*index=5*/...) all-reduce(f32[2,2,192]{2,1,0:T(2,128)S(1)} %pad_maximum_fusion.8, ...), channel_id=1, replica_groups=mesh['dp'=8,'grp'=4] {'dp'}, use_global_device_ids=true, to_apply=%region_35.36 | all-reduce | flops 8064 | bytes 64512 | tf_op jit(solution)/shard_map/psum | solution.py:376
  741.4 184.1 %all-reduce.12.cloned.1.call-done = (f32[2,1,192,576]{3,2,1,0:T(8,128)}, f32[2,768,768]{2,1,0:T(8,128)}, f32[2,1,192,768]{3,2,1,0:T(8,128)}, f32[2,1,768,192]{2,3,1,0:T(8,128)}) async-done(((f32[2,1,192,576]{3,2,1,0:T(8,128)}, f32[2,768,768]{2,1,0:T(8,128)}, f32[2,1,192,768]{3,2,1,0:T(8,128)}, f32[2,1,768,192]{2,3,1,0:T(8,128)}), (f32[2,1,192,576]{3,2,1,0:T(8,128)}, f32[2,768,768]{2,1,0:T(8,128)}, ...) | async-done | bytes 7962640 | tf_op jit(solution)/shard_map/psum | solution.py:376
  (458 shorter events, 366.9 us)
Async XLA Ops:
  7.2 16.0 %all-to-all-start = ((bf16[4,512,192]{1,2,0:T(8,128)(2,1)}), bf16[4,512,192]{1,2,0:T(8,128)(2,1)S(1)}, u32[]{:S(2)}, u32[]{:S(2)}) async-start(bf16[4,512,192]{1,2,0:T(8,128)(2,1)} %param.15), calls=%async_computation | async-start | bytes 1572864 | tf_op jit(solution)/shard_map/all_to_all | solution.py:142
  23.2 15.1 %all-to-all-start.3 = ((bf16[4,512,192]{1,2,0:T(8,128)(2,1)}), bf16[4,512,192]{1,2,0:T(8,128)(2,1)S(1)}, u32[]{:S(2)}, u32[]{:S(2)}) async-start(bf16[4,512,192]{1,2,0:T(8,128)(2,1)} %bitcast.407), calls=%async_computation.3 | async-start | bytes 1572864 | tf_op jit(solution)/shard_map/all_to_all | solution.py:140
  38.3 19.4 %copy-start.32 = (bf16[4,512,192]{1,2,0:T(8,128)(2,1)}, bf16[4,512,192]{1,2,0:T(8,128)(2,1)S(1)}, u32[]{:S(2)}) copy-start(bf16[4,512,192]{1,2,0:T(8,128)(2,1)S(1)} %all-to-all-done.3) | copy-start | bytes 2359300
  38.3 15.9 %all-to-all-start.2 = ((bf16[4,512,192]{1,2,0:T(8,128)(2,1)}), bf16[4,512,192]{1,2,0:T(8,128)(2,1)}, u32[]{:S(2)}, u32[]{:S(2)}) async-start(bf16[4,512,192]{1,2,0:T(8,128)(2,1)} %bitcast.408), calls=%async_computation.2 | async-start | bytes 1572864 | tf_op jit(solution)/shard_map/all_to_all | solution.py:139
  43.3 33.6 %copy-start.74 = (f32[768]{0:T(1024)}, f32[768]{0:T(1024)S(1)}, u32[]{:S(2)}) copy-start(f32[768]{0:T(1024)S(1)} %get-tuple-element.321) | copy-start | bytes 9220
  54.2 15.1 %all-to-all-start.1 = ((bf16[4,512,192]{1,2,0:T(8,128)(2,1)}), bf16[4,512,192]{1,2,0:T(8,128)(2,1)S(1)}, u32[]{:S(2)}, u32[]{:S(2)}) async-start(bf16[4,512,192]{1,2,0:T(8,128)(2,1)} %bitcast.409), calls=%async_computation.1 | async-start | bytes 1572864 | tf_op jit(solution)/shard_map/all_to_all | solution.py:141
  86.9 15.1 %all-to-all-start.4 = ((bf16[4,2,49152]{2,1,0:T(2,128)(2,1)}), bf16[4,2,49152]{2,1,0:T(2,128)(2,1)S(1)}, u32[]{:S(2)}, u32[]{:S(2)}) async-start(bf16[4,2,49152]{2,1,0:T(2,128)(2,1)} %reshape.507), calls=%async_computation.4 | async-start | bytes 1572864 | tf_op jit(solution)/shard_map/all_to_all | solution.py:162
  91.0 40.6 %copy-start.82 = (f32[1,192]{1,0:T(1,128)}, f32[1,192]{1,0:T(1,128)S(1)}, u32[]{:S(2)}) copy-start(f32[1,192]{1,0:T(1,128)S(1)} %get-tuple-element.293) | copy-start | bytes 2308
  103.7 15.9 %copy-start.47 = (bf16[24,8,4,512]{3,1,2,0:T(8,128)(2,1)}, bf16[24,8,4,512]{3,1,2,0:T(8,128)(2,1)S(1)}, u32[]{:S(2)}) copy-start(bf16[24,8,4,512]{3,1,2,0:T(8,128)(2,1)S(1)} %copy.218) | copy-start | bytes 2359300
  103.8 15.9 %copy-start.107 = (bf16[2,1,768,192]{2,3,1,0:T(8,128)(2,1)S(1)}, bf16[2,1,768,192]{2,3,1,0:T(8,128)(2,1)}, u32[]{:S(2)}) copy-start(bf16[2,1,768,192]{2,3,1,0:T(8,128)(2,1)} %param.26) | copy-start | bytes 1769476
  121.4 17.4 %copy-start.16 = (f32[2048,192]{0,1:T(8,128)}, f32[2048,192]{0,1:T(8,128)S(1)}, u32[]{:S(2)}) copy-start(f32[2048,192]{0,1:T(8,128)S(1)} %get-tuple-element.304) | copy-start | bytes 4718596
  133.5 15.1 %all-to-all-start.5 = ((bf16[4,512,192]{1,2,0:T(8,128)(2,1)}), bf16[4,512,192]{1,2,0:T(8,128)(2,1)S(1)}, u32[]{:S(2)}, u32[]{:S(2)}) async-start(bf16[4,512,192]{1,2,0:T(8,128)(2,1)} %bitcast.406), calls=%async_computation.5 | async-start | bytes 1572864 | tf_op jit(solution)/shard_map/all_to_all | solution.py:142
  148.7 15.3 %all-to-all-start.8 = ((bf16[4,512,192]{1,2,0:T(8,128)(2,1)}), bf16[4,512,192]{1,2,0:T(8,128)(2,1)S(1)}, u32[]{:S(2)}, u32[]{:S(2)}) async-start(bf16[4,512,192]{1,2,0:T(8,128)(2,1)} %bitcast.403), calls=%async_computation.8 | async-start | bytes 1572864 | tf_op jit(solution)/shard_map/all_to_all | solution.py:140
  164.0 19.4 %copy-start.34 = (bf16[4,512,192]{1,2,0:T(8,128)(2,1)}, bf16[4,512,192]{1,2,0:T(8,128)(2,1)S(1)}, u32[]{:S(2)}) copy-start(bf16[4,512,192]{1,2,0:T(8,128)(2,1)S(1)} %all-to-all-done.8) | copy-start | bytes 2359300
  164.0 15.9 %all-to-all-start.7 = ((bf16[4,512,192]{1,2,0:T(8,128)(2,1)}), bf16[4,512,192]{1,2,0:T(8,128)(2,1)}, u32[]{:S(2)}, u32[]{:S(2)}) async-start(bf16[4,512,192]{1,2,0:T(8,128)(2,1)} %bitcast.404), calls=%async_computation.7 | async-start | bytes 1572864 | tf_op jit(solution)/shard_map/all_to_all | solution.py:139
  179.9 15.1 %all-to-all-start.6 = ((bf16[4,512,192]{1,2,0:T(8,128)(2,1)}), bf16[4,512,192]{1,2,0:T(8,128)(2,1)S(1)}, u32[]{:S(2)}, u32[]{:S(2)}) async-start(bf16[4,512,192]{1,2,0:T(8,128)(2,1)} %bitcast.405), calls=%async_computation.6 | async-start | bytes 1572864 | tf_op jit(solution)/shard_map/all_to_all | solution.py:141
  216.3 15.9 %all-to-all-start.9 = ((bf16[4,2,49152]{2,1,0:T(2,128)(2,1)}), bf16[4,2,49152]{2,1,0:T(2,128)(2,1)}, u32[]{:S(2)}, u32[]{:S(2)}) async-start(bf16[4,2,49152]{2,1,0:T(2,128)(2,1)} %reshape.509), calls=%async_computation.9 | async-start | bytes 1572864 | tf_op jit(solution)/shard_map/all_to_all | solution.py:162
  221.9 45.1 %copy-start.14 = (f32[4,24,8,512]{3,2,0,1:T(8,128)}, f32[4,24,8,512]{3,2,0,1:T(8,128)S(1)}, u32[]{:S(2)}) copy-start(f32[4,24,8,512]{3,2,0,1:T(8,128)S(1)} %copy.217) | copy-start | bytes 4718596
  238.4 15.9 %copy-start.48 = (bf16[24,8,4,512]{3,1,2,0:T(8,128)(2,1)}, bf16[24,8,4,512]{3,1,2,0:T(8,128)(2,1)S(1)}, u32[]{:S(2)}) copy-start(bf16[24,8,4,512]{3,1,2,0:T(8,128)(2,1)S(1)} %copy.219) | copy-start | bytes 2359300
  256.7 23.0 %copy-start.98 = (f32[1,192]{1,0:T(1,128)S(1)}, f32[1,192]{1,0:T(1,128)}, u32[]{:S(2)}) copy-start(f32[1,192]{1,0:T(1,128)} %get-tuple-element.294) | copy-start | bytes 2308
  292.8 15.9 %all-to-all-start.10 = ((bf16[4,512,192]{1,2,0:T(8,128)(2,1)}), bf16[4,512,192]{1,2,0:T(8,128)(2,1)}, u32[]{:S(2)}, u32[]{:S(2)}) async-start(bf16[4,512,192]{1,2,0:T(8,128)(2,1)} %bitcast.474), calls=%async_computation.10 | async-start | bytes 1572864 | tf_op jit(solution)/shard_map/all_to_all | solution.py:258
  339.1 26.0 %all-to-all-start.13 = ((bf16[4,2,49152]{2,1,0:T(2,128)(2,1)}), bf16[4,2,49152]{2,1,0:T(2,128)(2,1)S(1)}, u32[]{:S(2)}, u32[]{:S(2)}) async-start(bf16[4,2,49152]{2,1,0:T(2,128)(2,1)} %reshape.517), calls=%async_computation.13 | async-start | bytes 1572864 | tf_op jit(solution)/shard_map/all_to_all | solution.py:286
  365.0 28.2 %all-to-all-start.14 = ((bf16[4,2,49152]{2,1,0:T(2,128)(2,1)}), bf16[4,2,49152]{2,1,0:T(2,128)(2,1)}, u32[]{:S(2)}, u32[]{:S(2)}) async-start(bf16[4,2,49152]{2,1,0:T(2,128)(2,1)} %reshape.511), calls=%async_computation.14 | async-start | bytes 1572864 | tf_op jit(solution)/shard_map/all_to_all | solution.py:287
  393.2 18.5 %all-to-all-start.12 = ((bf16[4,2,49152]{2,1,0:T(2,128)(2,1)}), bf16[4,2,49152]{2,1,0:T(2,128)(2,1)}, u32[]{:S(2)}, u32[]{:S(2)}) async-start(bf16[4,2,49152]{2,1,0:T(2,128)(2,1)} %reshape.515), calls=%async_computation.12 | async-start | bytes 1572864 | tf_op jit(solution)/shard_map/all_to_all | solution.py:285
  411.7 22.0 %all-to-all-start.11 = ((bf16[4,2,49152]{2,1,0:T(2,128)(2,1)}), bf16[4,2,49152]{2,1,0:T(2,128)(2,1)}, u32[]{:S(2)}, u32[]{:S(2)}) async-start(bf16[4,2,49152]{2,1,0:T(2,128)(2,1)} %reshape.513), calls=%async_computation.11 | async-start | bytes 1572864 | tf_op jit(solution)/shard_map/all_to_all | solution.py:284
  463.8 16.3 %all-to-all-start.15 = ((bf16[4,512,192]{1,2,0:T(8,128)(2,1)}), bf16[4,512,192]{1,2,0:T(8,128)(2,1)}, u32[]{:S(2)}, u32[]{:S(2)}) async-start(bf16[4,512,192]{1,2,0:T(8,128)(2,1)} %bitcast.473), calls=%async_computation.15 | async-start | bytes 1572864 | tf_op jit(solution)/shard_map/all_to_all | solution.py:258
  512.8 29.3 %all-to-all-start.18 = ((bf16[4,2,49152]{2,1,0:T(2,128)(2,1)}), bf16[4,2,49152]{2,1,0:T(2,128)(2,1)}, u32[]{:S(2)}, u32[]{:S(2)}) async-start(bf16[4,2,49152]{2,1,0:T(2,128)(2,1)} %reshape.525), calls=%async_computation.18 | async-start | bytes 1572864 | tf_op jit(solution)/shard_map/all_to_all | solution.py:286
  542.0 26.4 %all-to-all-start.17 = ((bf16[4,2,49152]{2,1,0:T(2,128)(2,1)}), bf16[4,2,49152]{2,1,0:T(2,128)(2,1)}, u32[]{:S(2)}, u32[]{:S(2)}) async-start(bf16[4,2,49152]{2,1,0:T(2,128)(2,1)} %reshape.523), calls=%async_computation.17 | async-start | bytes 1572864 | tf_op jit(solution)/shard_map/all_to_all | solution.py:285
  546.2 109.5 %all-reduce.10.cloned.1.call-start = ((), (), s32[]{:S(2)}) async-start(), calls=%async_computation.20 | async-start | bytes 9437184 | tf_op jit(solution)/shard_map/psum | solution.py:13
  568.5 24.8 %all-to-all-start.16 = ((bf16[4,2,49152]{2,1,0:T(2,128)(2,1)}), bf16[4,2,49152]{2,1,0:T(2,128)(2,1)}, u32[]{:S(2)}, u32[]{:S(2)}) async-start(bf16[4,2,49152]{2,1,0:T(2,128)(2,1)} %reshape.521), calls=%async_computation.16 | async-start | bytes 1572864 | tf_op jit(solution)/shard_map/all_to_all | solution.py:284
  572.7 352.9 %all-reduce.12.cloned.1.call-start = ((), (), s32[]{:S(2)}) async-start(), calls=%async_computation.21 | async-start | bytes 16121856 | tf_op jit(solution)/shard_map/psum | solution.py:376
  671.2 22.3 %all-to-all-start.19 = ((bf16[4,2,49152]{2,1,0:T(2,128)(2,1)}), bf16[4,2,49152]{2,1,0:T(2,128)(2,1)}, u32[]{:S(2)}, u32[]{:S(2)}) async-start(bf16[4,2,49152]{2,1,0:T(2,128)(2,1)} %reshape.519), calls=%async_computation.19 | async-start | bytes 1572864 | tf_op jit(solution)/shard_map/all_to_all | solution.py:287
  (101 other events, 547.8 us)
Sparse Core Ops, SparseCore 0:
  550.8 104.8 all-reduce.9
  661.3 264.1 all-reduce.11
